TPU v7x, 256 devices: a whole 4x4x8 slice. The times are simulated.
256 devices in a mesh: tm: 128 (over z, y, x), rhs: 2 (over core).
Axes of the slice: x: 4, y: 4, z: 8, core: 2. Of those that a mesh axis runs over, the one named last changes fastest.
Arguments:
- diag: float32 [262144, 512], P('tm', 'rhs'), as said below
- lower: float32 [262144, 512], P('tm', 'rhs'), as said below
- right_side: float32 [128, 262144], P('rhs', 'tm'), may hold values from -6 to 6
- coarse_sol: float32 [128, 65536], P('rhs', 'tm'), may hold values from -6 to 6
Outputs:
- coarse_diag: float32 [65536, 512], P('tm', 'rhs')
- coarse_lower: float32 [65536, 512], P('tm', 'rhs')
- coarse_rhs: float32 [128, 65536], P('rhs', 'tm')
- solution: float32 [128, 262144], P('rhs', 'tm')
Inputs may be any that keep to these rules, and one draw needn't show every extreme that they name: diag and lower are the diagonal and coupling blocks of a symmetric positive definite periodic block tridiagonal matrix whose eigenvalues are all at least 2; every diagonal block is symmetric. lower holds the coupling blocks of the matrix described for diag.
All inputs are finite; a program needn't handle non-finite values.
Results may differ from a plain program's by a relative error of at most 0.0003.
Values sent between devices are 32-bit elements; how exact they have to be, the bound alone decides.
A program may use at most 128 MiB of HBM per device.

v0:
```python
import jax
import jax.numpy as jnp
from jax import lax
from jax.sharding import PartitionSpec as P


def shifted(shard, axis, by):
    size = lax.axis_size(axis)
    return lax.ppermute(shard, axis, [(i, (i + by) % size) for i in range(size)])


def product(first_term, second_term):
    return jnp.dot(
        first_term, second_term, precision=lax.Precision.HIGHEST, preferred_element_type=jnp.float32
    )


def apply_inverse(factor, stacked):
    halfway = lax.linalg.triangular_solve(factor, stacked, left_side=True, lower=True)
    return lax.linalg.triangular_solve(
        factor, halfway, left_side=True, lower=True, transpose_a=True
    )


def slice_cols(matrix, first_col, col_count):
    return lax.dynamic_slice_in_dim(matrix, first_col, col_count, 1)


def slice_rows(matrix, first_row, row_count):
    return lax.dynamic_slice_in_dim(matrix, first_row, row_count, 0)


def eliminate_one(diag_block, link_block, next_link, rhs_block, first_col, col_count):
    factor = jnp.linalg.cholesky(diag_block)
    stacked = jnp.concatenate(
        [
            slice_cols(link_block, first_col, col_count),
            slice_rows(next_link, first_col, col_count).T,
            rhs_block,
        ],
        axis=1,
    )
    solved = apply_inverse(factor, stacked)
    return (
        factor,
        solved[:, :col_count],
        solved[:, col_count : 2 * col_count],
        solved[:, 2 * col_count :],
    )


def shards(diag, lower, right_side, coarse_sol):
    span_cols = diag.shape[1]
    block_order = span_cols * lax.axis_size("rhs")
    column_start = lax.axis_index("rhs") * span_cols
    next_share = shifted(lower[:block_order], "tm", -1)
    full_diag, full_lower, next_lower = (
        lax.all_gather(diag, "rhs", axis=1, tiled=True),
        lax.all_gather(lower, "rhs", axis=1, tiled=True),
        lax.all_gather(next_share, "rhs", axis=1, tiled=True),
    )
    diag_blocks = [
        full_diag[position * block_order : (position + 1) * block_order] for position in range(4)
    ]
    link_blocks = [
        full_lower[position * block_order : (position + 1) * block_order] for position in range(4)
    ]
    rhs_blocks = [
        right_side[:, position * block_order : (position + 1) * block_order].T
        for position in range(4)
    ]
    factor_one, prev_one, next_one, own_one = eliminate_one(
        diag_blocks[1], link_blocks[1], link_blocks[2], rhs_blocks[1], column_start, span_cols
    )
    factor_three, prev_three, next_three, own_three = eliminate_one(
        diag_blocks[3], link_blocks[3], next_lower, rhs_blocks[3], column_start, span_cols
    )
    came_prev, came_next, came_own = shifted((prev_three, next_three, own_three), "tm", 1)
    kept_diag = (
        slice_cols(diag_blocks[0], column_start, span_cols)
        - product(link_blocks[1].T, prev_one)
        - product(link_blocks[0], came_next)
    )
    kept_link = -product(link_blocks[0], came_prev)
    kept_rhs = (
        rhs_blocks[0] - product(link_blocks[1].T, own_one) - product(link_blocks[0], came_own)
    )
    odd_diag = (
        slice_cols(diag_blocks[2], column_start, span_cols)
        - product(link_blocks[3].T, prev_three)
        - product(link_blocks[2], next_one)
    )
    odd_link = -product(link_blocks[2], prev_one)
    odd_rhs = (
        rhs_blocks[2] - product(link_blocks[3].T, own_three) - product(link_blocks[2], own_one)
    )
    next_piece = shifted(kept_link, "tm", -1)
    odd_full, kept_link_full, odd_link_full, following = (
        lax.all_gather(odd_diag, "rhs", axis=1, tiled=True),
        lax.all_gather(kept_link, "rhs", axis=1, tiled=True),
        lax.all_gather(odd_link, "rhs", axis=1, tiled=True),
        lax.all_gather(next_piece, "rhs", axis=1, tiled=True),
    )
    factor_odd, prev_two, next_two, own_two = eliminate_one(
        odd_full, odd_link_full, following, odd_rhs, column_start, span_cols
    )
    came_prev_two, came_next_two, came_own_two = shifted((prev_two, next_two, own_two), "tm", 1)
    coarse_diag = (
        kept_diag - product(odd_link_full.T, prev_two) - product(kept_link_full, came_next_two)
    )
    coarse_lower = -product(kept_link_full, came_prev_two)
    coarse_rhs = (
        kept_rhs - product(odd_link_full.T, own_two) - product(kept_link_full, came_own_two)
    )
    kept_values = coarse_sol.T
    later_values = shifted(coarse_sol, "tm", -1).T
    odd_values = apply_inverse(
        factor_odd,
        odd_rhs - product(odd_link_full, kept_values) - product(following.T, later_values),
    )
    first_values = apply_inverse(
        factor_one,
        rhs_blocks[1]
        - product(link_blocks[1], kept_values)
        - product(link_blocks[2].T, odd_values),
    )
    third_values = apply_inverse(
        factor_three,
        rhs_blocks[3] - product(link_blocks[3], odd_values) - product(next_lower.T, later_values),
    )
    solution = jnp.concatenate([kept_values, first_values, odd_values, third_values], axis=0).T
    return (coarse_diag, coarse_lower, coarse_rhs.T, solution)


def solution(mesh):
    return jax.shard_map(
        shards,
        mesh=mesh,
        in_specs=(P("tm", "rhs"), P("tm", "rhs"), P("rhs", "tm"), P("rhs", "tm")),
        out_specs=(P("tm", "rhs"), P("tm", "rhs"), P("rhs", "tm"), P("rhs", "tm")),
        check_vma=False,
    )
```

profile of v0, /device:TPU:0, one launch (start us, length us, event | category | flops | bytes accessed | tf_op | source)
XLA Modules:
  0.0 676.5 jit_solution(9035725231035911094)
XLA Ops:
  8.3 8.9 %collective-permute-start = (f32[512,256]{1,0:T(8,128)S(1)}, f32[512,256]{1,0:T(8,128)S(1)}, u32[]{:S(2)}, u32[]{:S(2)}) collective-permute-start(f32[512,256]{1,0:T(8,128)S(1)} %slice.264), channel_id=1, source_target_pairs={{0,254},{2,0},{4,2},{6,4},{8,6},{10,8},{12,10},{14,12},{16,14},{18... | collective-permute-start | bytes 1572872 | tf_op jit(solution)/shard_map/ppermute | solution.py:9
  17.2 11.2 %collective-permute-done = f32[512,256]{1,0:T(8,128)S(1)} collective-permute-done((f32[512,256]{1,0:T(8,128)S(1)}, f32[512,256]{1,0:T(8,128)S(1)}, u32[]{:S(2)}, u32[]{:S(2)}) %collective-permute-start) | collective-permute-done | bytes 524320 | tf_op jit(solution)/shard_map/ppermute | solution.py:9
  29.2 2.9 copy.8
  33.7 1.9 copy.10
  38.1 4.5 all-gather.12.cloned.1.call-done
  42.7 1.9 dynamic-slice_bitcast_fusion.1
  44.5 20.3 %all-gather.8.cloned.1.call-done = f32[2048,512]{0,1:T(8,128)} async-done(((f32[2048,256]{0,1:T(8,128)}), f32[2048,512]{0,1:T(8,128)}) %all-gather.8.cloned.1.call-update) | async-done | bytes 4194320 | tf_op jit(solution)/shard_map/all_gather | solution.py:58
  64.8 4.1 fusion.293
  69.6 3.0 fusion.12
  72.6 11.7 %cholesky.374 = f32[128,128]{1,0:T(8,128)S(1)} custom-call(f32[128,128]{1,0:T(8,128)S(1)} %cholesky.586), custom_call_target="Cholesky" | custom-call | tf_op jit(solution)/shard_map/jit(cholesky)/cholesky | solution.py:34
  84.4 9.8 %custom-call.46 = f32[1,128,128]{1,2,0:T(8,128)S(1)} custom-call(f32[1,128,128]{2,1,0:T(8,128)S(1)} %get-tuple-element.179), custom_call_target="InvertDiagBlocksLowerTriangular" | custom-call | tf_op jit(solution)/shard_map/jit(cholesky)/cholesky | solution.py:34
  95.0 11.9 %cholesky.393 = f32[128,128]{1,0:T(8,128)S(1)} custom-call(f32[128,128]{1,0:T(8,128)S(1)} %cholesky.590), custom_call_target="Cholesky" | custom-call | tf_op jit(solution)/shard_map/jit(cholesky)/cholesky | solution.py:34
  106.9 9.8 %custom-call.47 = f32[1,128,128]{1,2,0:T(8,128)S(1)} custom-call(f32[1,128,128]{2,1,0:T(8,128)S(1)} %get-tuple-element.176), custom_call_target="InvertDiagBlocksLowerTriangular" | custom-call | tf_op jit(solution)/shard_map/jit(cholesky)/cholesky | solution.py:34
  117.4 11.7 %cholesky.414 = f32[128,128]{1,0:T(8,128)S(1)} custom-call(f32[128,128]{1,0:T(8,128)S(1)} %cholesky.595), custom_call_target="Cholesky" | custom-call | tf_op jit(solution)/shard_map/jit(cholesky)/cholesky | solution.py:34
  129.2 9.8 %custom-call.48 = f32[1,128,128]{1,2,0:T(8,128)S(1)} custom-call(f32[1,128,128]{2,1,0:T(8,128)S(1)} %get-tuple-element.173), custom_call_target="InvertDiagBlocksLowerTriangular" | custom-call | tf_op jit(solution)/shard_map/jit(cholesky)/cholesky | solution.py:34
  139.6 22.7 %cholesky.431 = f32[128,128]{1,0:T(8,128)S(1)} custom-call(f32[128,128]{1,0:T(8,128)S(1)} %convolution_subtract_fusion.30), custom_call_target="Cholesky" | custom-call | tf_op jit(solution)/shard_map/jit(cholesky)/cholesky | solution.py:34
  167.2 8.0 %while.24 = (s32[]{:T(128)}, f32[512,512]{1,0:T(8,128)S(1)}, s32[4,2]{0,1:T(2,128)S(1)}, f32[4,128,128]{2,1,0:T(8,128)S(1)}, s32[]{:T(128)}) while((s32[]{:T(128)}, f32[512,512]{1,0:T(8,128)S(1)}, s32[4,2]{0,1:T(2,128)S(1)}, f32[4,128,128]{2,1,0:T(8,128)S(1)}, s32[]{:T(128)}) %tuple.120), condition=%wide.while_cond.1, body=%wide.while_body.1.sunk | while | flops 2 | bytes 131181 | solution.py:20
  175.2 39.3 %custom-call.50 = f32[4,128,128]{1,2,0:T(8,128)S(1)} custom-call(f32[4,128,128]{2,1,0:T(8,128)S(1)} %get-tuple-element.90), custom_call_target="InvertDiagBlocksLowerTriangular" | custom-call | tf_op jit(solution)/shard_map/triangular_solve/custom-call.8 | solution.py:20
  214.5 3.2 fusion.294
  229.2 12.1 %cholesky.446 = f32[128,128]{1,0:T(8,128)S(1)} custom-call(f32[128,128]{1,0:T(8,128)S(1)} %cholesky.599), custom_call_target="Cholesky" | custom-call | tf_op jit(solution)/shard_map/jit(cholesky)/cholesky | solution.py:34
  241.3 9.8 %custom-call.51 = f32[1,128,128]{1,2,0:T(8,128)S(1)} custom-call(f32[1,128,128]{2,1,0:T(8,128)S(1)} %get-tuple-element.169), custom_call_target="InvertDiagBlocksLowerTriangular" | custom-call | tf_op jit(solution)/shard_map/jit(cholesky)/cholesky | solution.py:34
  253.8 11.7 %cholesky.465 = f32[128,128]{1,0:T(8,128)S(1)} custom-call(f32[128,128]{1,0:T(8,128)S(1)} %cholesky.603), custom_call_target="Cholesky" | custom-call | tf_op jit(solution)/shard_map/jit(cholesky)/cholesky | solution.py:34
  265.5 9.8 %custom-call.52 = f32[1,128,128]{1,2,0:T(8,128)S(1)} custom-call(f32[1,128,128]{2,1,0:T(8,128)S(1)} %get-tuple-element.166), custom_call_target="InvertDiagBlocksLowerTriangular" | custom-call | tf_op jit(solution)/shard_map/jit(cholesky)/cholesky | solution.py:34
  276.9 11.9 %cholesky.486 = f32[128,128]{1,0:T(8,128)S(1)} custom-call(f32[128,128]{1,0:T(8,128)S(1)} %cholesky.608), custom_call_target="Cholesky" | custom-call | tf_op jit(solution)/shard_map/jit(cholesky)/cholesky | solution.py:34
  289.5 9.8 %custom-call.53 = f32[1,128,128]{1,2,0:T(8,128)S(1)} custom-call(f32[1,128,128]{2,1,0:T(8,128)S(1)} %get-tuple-element.163), custom_call_target="InvertDiagBlocksLowerTriangular" | custom-call | tf_op jit(solution)/shard_map/jit(cholesky)/cholesky | solution.py:34
  300.7 11.7 %cholesky.503 = f32[128,128]{1,0:T(8,128)S(1)} custom-call(f32[128,128]{1,0:T(8,128)S(1)} %convolution_subtract_fusion.29), custom_call_target="Cholesky" | custom-call | tf_op jit(solution)/shard_map/jit(cholesky)/cholesky | solution.py:34
  317.8 8.0 %while.25 = (s32[]{:T(128)}, f32[512,512]{1,0:T(8,128)S(1)}, s32[4,2]{0,1:T(2,128)S(1)}, f32[4,128,128]{2,1,0:T(8,128)S(1)}, s32[]{:T(128)}) while((s32[]{:T(128)}, f32[512,512]{1,0:T(8,128)S(1)}, s32[4,2]{0,1:T(2,128)S(1)}, f32[4,128,128]{2,1,0:T(8,128)S(1)}, s32[]{:T(128)}) %tuple.143), condition=%wide.while_cond.1.clone, body=%wide.while_body.1.clone.sunk | while | flops 2 | bytes 131181 | solution.py:20
  326.5 40.5 %custom-call.55 = f32[4,128,128]{1,2,0:T(8,128)S(1)} custom-call(f32[4,128,128]{2,1,0:T(8,128)} %copy-done.45), custom_call_target="InvertDiagBlocksLowerTriangular" | custom-call | tf_op jit(solution)/shard_map/triangular_solve/custom-call.8 | solution.py:20
  377.4 2.4 copy-done
  380.8 1.9 fusion.1
  382.8 2.2 fusion.296
  386.3 3.2 fusion.3
  389.6 15.5 %collective-permute-done.2 = f32[512,256]{0,1:T(8,128)} collective-permute-done((f32[512,256]{0,1:T(8,128)}, f32[512,256]{0,1:T(8,128)}, u32[]{:S(2)}, u32[]{:S(2)}) %collective-permute-start.2) | collective-permute-done | bytes 524320 | tf_op jit(solution)/shard_map/ppermute | solution.py:9
  405.1 4.0 fusion
  414.6 2.6 convolution_subtract_fusion.27
  417.2 7.0 %collective-permute-done.3 = f32[512,256]{1,0:T(8,128)} collective-permute-done((f32[512,256]{1,0:T(8,128)}, f32[512,256]{1,0:T(8,128)}, u32[]{:S(2)}, u32[]{:S(2)}) %collective-permute-start.3) | collective-permute-done | bytes 524320 | tf_op jit(solution)/shard_map/ppermute | solution.py:9
  424.5 2.7 convolution_subtract_fusion.22
  427.1 3.1 convolution_subtract_fusion.25
  430.2 2.0 fusion.9
  432.2 3.3 fusion.6
  435.5 2.8 copy.14
  440.8 11.7 %cholesky.518 = f32[128,128]{1,0:T(8,128)S(1)} custom-call(f32[128,128]{1,0:T(8,128)S(1)} %cholesky.612), custom_call_target="Cholesky" | custom-call | tf_op jit(solution)/shard_map/jit(cholesky)/cholesky | solution.py:34
  454.8 11.3 %custom-call.56 = f32[1,128,128]{1,2,0:T(8,128)} custom-call(f32[1,128,128]{2,1,0:T(8,128)} %get-tuple-element.159), custom_call_target="InvertDiagBlocksLowerTriangular" | custom-call | tf_op jit(solution)/shard_map/jit(cholesky)/cholesky | solution.py:34
  469.9 13.6 %cholesky.537 = f32[128,128]{1,0:T(8,128)} custom-call(f32[128,128]{1,0:T(8,128)} %cholesky.616), custom_call_target="Cholesky" | custom-call | tf_op jit(solution)/shard_map/jit(cholesky)/cholesky | solution.py:34
  486.3 11.3 %custom-call.57 = f32[1,128,128]{1,2,0:T(8,128)} custom-call(f32[1,128,128]{2,1,0:T(8,128)} %get-tuple-element.156), custom_call_target="InvertDiagBlocksLowerTriangular" | custom-call | tf_op jit(solution)/shard_map/jit(cholesky)/cholesky | solution.py:34
  501.3 13.2 %cholesky.558 = f32[128,128]{1,0:T(8,128)} custom-call(f32[128,128]{1,0:T(8,128)} %cholesky.621), custom_call_target="Cholesky" | custom-call | tf_op jit(solution)/shard_map/jit(cholesky)/cholesky | solution.py:34
  516.6 11.3 %custom-call.58 = f32[1,128,128]{1,2,0:T(8,128)} custom-call(f32[1,128,128]{2,1,0:T(8,128)} %get-tuple-element.153), custom_call_target="InvertDiagBlocksLowerTriangular" | custom-call | tf_op jit(solution)/shard_map/jit(cholesky)/cholesky | solution.py:34
  530.8 13.3 %cholesky.575 = f32[128,128]{1,0:T(8,128)} custom-call(f32[128,128]{1,0:T(8,128)} %convolution_subtract_fusion.28), custom_call_target="Cholesky" | custom-call | tf_op jit(solution)/shard_map/jit(cholesky)/cholesky | solution.py:34
  550.5 10.2 %while.26 = (s32[]{:T(128)}, f32[512,512]{1,0:T(8,128)S(1)}, s32[4,2]{0,1:T(2,128)S(1)}, f32[4,128,128]{2,1,0:T(8,128)}, s32[]{:T(128)}) while((s32[]{:T(128)}, f32[512,512]{1,0:T(8,128)S(1)}, s32[4,2]{0,1:T(2,128)S(1)}, f32[4,128,128]{2,1,0:T(8,128)}, s32[]{:T(128)}) %tuple.144), condition=%wide.while_cond.1.clone.1, body=%wide.while_body.1.clone.1.sunk | while | flops 2 | bytes 132705 | solution.py:20
  551.1 1.9 bitcast_dynamic-update-slice_fusion.8
  553.7 1.9 bitcast_dynamic-update-slice_fusion.8
  556.2 1.9 bitcast_dynamic-update-slice_fusion.8
  558.8 1.9 bitcast_dynamic-update-slice_fusion.8
  560.7 40.8 %custom-call.60 = f32[4,128,128]{1,2,0:T(8,128)} custom-call(f32[4,128,128]{2,1,0:T(8,128)} %get-tuple-element.94), custom_call_target="InvertDiagBlocksLowerTriangular" | custom-call | tf_op jit(solution)/shard_map/triangular_solve/custom-call.8 | solution.py:20
  601.5 2.0 constant_dynamic-slice_fusion.3
  603.5 2.4 convolution_subtract_fusion.21
  616.3 2.0 convolution_subtract_fusion.20
  633.4 2.0 fusion.297
  635.7 2.3 fusion.10
  639.6 2.1 fusion.5
  644.4 3.1 convolution_subtract_fusion.23
  647.5 15.8 %collective-permute-done.4 = f32[512,256]{0,1:T(8,128)} collective-permute-done((f32[512,256]{0,1:T(8,128)S(1)}, f32[512,256]{0,1:T(8,128)}, u32[]{:S(2)}, u32[]{:S(2)}) %collective-permute-start.4) | collective-permute-done | bytes 524320 | tf_op jit(solution)/shard_map/ppermute | solution.py:9
  663.3 2.1 convolution_subtract_fusion
  666.4 2.9 convolution_negate_fusion
  (327 shorter events, 123.6 us)
Async XLA Ops:
  7.2 35.5 %all-gather.12.cloned.1.call-start = ((), (), s32[]{:S(2)}) async-start(), calls=%async_computation.2 | async-start | bytes 1572864 | tf_op jit(solution)/shard_map/all_gather | solution.py:60
  8.3 20.1 %collective-permute-start = (f32[512,256]{1,0:T(8,128)S(1)}, f32[512,256]{1,0:T(8,128)S(1)}, u32[]{:S(2)}, u32[]{:S(2)}) collective-permute-start(f32[512,256]{1,0:T(8,128)S(1)} %slice.264), channel_id=1, source_target_pairs={{0,254},{2,0},{4,2},{6,4},{8,6},{10,8},{12,10},{14,12},{16,14},{18... | collective-permute-start | bytes 1572872 | tf_op jit(solution)/shard_map/ppermute | solution.py:9
  28.3 0.8 copy-start.38
  29.2 35.6 %all-gather.8.cloned.1.call-start = ((), (), s32[]{:S(2)}) async-start(), calls=%async_computation | async-start | bytes 6291456 | tf_op jit(solution)/shard_map/all_gather | solution.py:58
  32.1 1.6 copy-start.19
  32.2 182.4 %all-gather.10.cloned.1.call-start = ((), (), s32[]{:S(2)}) async-start(), calls=%async_computation.1 | async-start | bytes 6291456 | tf_op jit(solution)/shard_map/all_gather | solution.py:59
  35.6 1.0 copy-start.31
  35.6 399.9 %all-gather.16.cloned.1.call-start = ((), (), s32[]{:S(2)}) async-start(), calls=%async_computation.4 | async-start | bytes 1572864 | tf_op jit(solution)/shard_map/all_gather | solution.py:99
  218.0 1.0 copy-start.35
  226.4 2.8 copy-start.10
  312.5 3.9 copy-start.7
  317.7 50.5 %copy-start.39 = (f32[512,64]{0,1:T(8,128)S(1)}, f32[512,64]{0,1:T(8,128)}, u32[]{:S(2)}) copy-start(f32[512,64]{0,1:T(8,128)} %get-tuple-element.148) | copy-start | bytes 393220
  325.8 0.7 copy-start.45
  367.0 5.0 copy-start.15
  367.1 1.3 copy-start.28
  372.8 2.0 copy-start.16
  375.2 1.4 copy-start.13
  375.2 1.3 copy-start.11
  375.2 1.3 copy-start.21
  376.1 1.3 copy-start.27
  376.5 0.7 copy-start.23
  376.5 3.2 copy-start
  377.3 3.6 copy-start.8
  377.4 3.5 copy-start.9
  382.8 218.7 %all-gather.14.cloned.1.call-start = ((), (), s32[]{:S(2)}) async-start(), calls=%async_computation.3 | async-start | bytes 1572864 | tf_op jit(solution)/shard_map/all_gather | solution.py:101
  385.1 20.0 %collective-permute-start.2 = (f32[512,256]{0,1:T(8,128)}, f32[512,256]{0,1:T(8,128)}, u32[]{:S(2)}, u32[]{:S(2)}) collective-permute-start(f32[512,256]{0,1:T(8,128)} %get-tuple-element.147), channel_id=1, source_target_pairs={{0,2},{2,4},{4,6},{6,8},{8,10},{10,12},{12,14},{14,16},{16,18},{18... | collective-permute-start | bytes 1572872 | tf_op jit(solution)/shard_map/ppermute | solution.py:9
  389.5 216.3 %all-gather.18.cloned.1.call-start = ((), (), s32[]{:S(2)}) async-start(), calls=%async_computation.5 | async-start | bytes 1572864 | tf_op jit(solution)/shard_map/all_gather | solution.py:102
  409.1 5.5 copy-start.12
  409.1 5.5 copy-start.22
  409.1 15.1 %collective-permute-start.3 = (f32[512,256]{1,0:T(8,128)}, f32[512,256]{1,0:T(8,128)}, u32[]{:S(2)}, u32[]{:S(2)}) collective-permute-start(f32[512,256]{1,0:T(8,128)} %fusion), channel_id=1, source_target_pairs={{0,254},{2,0},{4,2},{6,4},{8,6},{10,8},{12,10},{14,12},{16,14},{18... | collective-permute-start | bytes 1572872 | tf_op jit(solution)/shard_map/ppermute | solution.py:9
  410.8 205.0 %collective-permute-start.8 = (f32[64,512]{1,0:T(8,128)}, f32[64,512]{1,0:T(8,128)}, u32[]{:S(2)}, u32[]{:S(2)}) collective-permute-start(f32[64,512]{1,0:T(8,128)} %param.16), channel_id=1, source_target_pairs={{0,254},{2,0},{4,2},{6,4},{8,6},{10,8},{12,10},{14,12},{16,14},{18... | collective-permute-start | bytes 393224 | tf_op jit(solution)/shard_map/ppermute | solution.py:9
  413.1 222.5 %collective-permute-start.6 = (f32[512,64]{0,1:T(8,128)}, f32[512,64]{0,1:T(8,128)}, u32[]{:S(2)}, u32[]{:S(2)}) collective-permute-start(f32[512,64]{0,1:T(8,128)} %pad_maximum_fusion.8), channel_id=1, source_target_pairs={{0,2},{2,4},{4,6},{6,8},{8,10},{10,12},{12,14},{14,16},{16,18},{18... | collective-permute-start | bytes 393224 | tf_op jit(solution)/shard_map/ppermute | solution.py:9
  414.3 225.3 %collective-permute-start.1 = (f32[512,256]{0,1:T(8,128)}, f32[512,256]{0,1:T(8,128)}, u32[]{:S(2)}, u32[]{:S(2)}) collective-permute-start(f32[512,256]{0,1:T(8,128)} %get-tuple-element.146), channel_id=1, source_target_pairs={{0,2},{2,4},{4,6},{6,8},{8,10},{10,12},{12,14},{14,16},{16,18},{18... | collective-permute-start | bytes 1572872 | tf_op jit(solution)/shard_map/ppermute | solution.py:9
  414.6 9.9 %copy-start.32 = (f32[64,2048]{1,0:T(8,128)S(1)}, f32[64,2048]{1,0:T(8,128)}, u32[]{:S(2)}) copy-start(f32[64,2048]{1,0:T(8,128)} %param.15) | copy-start | bytes 1572868
  414.6 9.9 %copy-start.33 = (f32[64,512]{1,0:T(8,128)S(1)}, f32[64,512]{1,0:T(8,128)}, u32[]{:S(2)}) copy-start(f32[64,512]{1,0:T(8,128)} %param.16) | copy-start | bytes 393220
  424.2 218.6 %all-gather.20.cloned.1.call-start = ((), (), s32[]{:S(2)}) async-start(), calls=%async_computation.6 | async-start | bytes 1572864 | tf_op jit(solution)/shard_map/all_gather | solution.py:100
  427.1 5.0 copy-start.26
  435.5 2.8 copy-start.14
  439.7 1.1 copy-start.20
  452.6 0.6 copy-start.44
  468.6 0.7 copy-start.36
  500.0 0.7 copy-start.37
  545.0 3.4 copy-start.6
  560.7 40.8 %copy-start.4 = (f32[512,512]{1,0:T(8,128)}, f32[512,512]{1,0:T(8,128)S(1)}, u32[]{:S(2)}) copy-start(f32[512,512]{1,0:T(8,128)S(1)} %get-tuple-element.339) | copy-start | bytes 3145732
  601.5 2.0 copy-start.2
  605.8 1.2 copy-start.30
  607.0 0.9 copy-start.18
  607.0 1.3 copy-start.5
  615.1 1.3 copy-start.25
  615.1 1.3 copy-start.43
  615.7 5.9 copy-start.1
  618.8 2.9 copy-start.42
  624.3 3.0 copy-start.24
  625.6 3.4 copy-start.17
  632.2 12.2 %collective-permute-start.7 = (f32[512,64]{0,1:T(8,128)}, f32[512,64]{0,1:T(8,128)}, u32[]{:S(2)}, u32[]{:S(2)}) collective-permute-start(f32[512,64]{0,1:T(8,128)} %pad_maximum_fusion.6), channel_id=1, source_target_pairs={{0,2},{2,4},{4,6},{6,8},{8,10},{10,12},{12,14},{14,16},{16,18},{18... | collective-permute-start | bytes 393224 | tf_op jit(solution)/shard_map/ppermute | solution.py:9
  633.2 2.5 copy-start.40
  633.2 33.3 %collective-permute-start.5 = (f32[512,256]{0,1:T(8,128)}, f32[512,256]{0,1:T(8,128)}, u32[]{:S(2)}, u32[]{:S(2)}) collective-permute-start(f32[512,256]{0,1:T(8,128)} %get-tuple-element.144), channel_id=1, source_target_pairs={{0,2},{2,4},{4,6},{6,8},{8,10},{10,12},{12,14},{14,16},{16,18},{18... | collective-permute-start | bytes 1572872 | tf_op jit(solution)/shard_map/ppermute | solution.py:9
  633.2 30.1 %collective-permute-start.4 = (f32[512,256]{0,1:T(8,128)S(1)}, f32[512,256]{0,1:T(8,128)}, u32[]{:S(2)}, u32[]{:S(2)}) collective-permute-start(f32[512,256]{0,1:T(8,128)S(1)} %get-tuple-element.145), channel_id=1, source_target_pairs={{0,2},{2,4},{4,6},{6,8},{8,10},{10,12},{12,14},{14,16},{16,18},{18... | collective-permute-start | bytes 1572872 | tf_op jit(solution)/shard_map/ppermute | solution.py:9
  638.2 1.4 copy-start.29
  639.6 2.4 copy-start.34
  641.8 2.6 copy-start.41
  642.9 20.4 %copy-start.3 = (f32[512,512]{1,0:T(8,128)S(1)}, f32[512,512]{1,0:T(8,128)}, u32[]{:S(2)}) copy-start(f32[512,512]{1,0:T(8,128)} %all-gather.20.cloned.1.call-done) | copy-start | bytes 3145732
Sparse Core Ops, SparseCore 0:
  29.3 13.3 all-gather.11
  44.5 20.2 all-gather.7
  66.6 20.4 all-gather.9
  382.9 15.6 all-gather.15
  400.8 15.6 all-gather.13
  424.3 13.5 all-gather.17
  440.3 15.7 all-gather.19
where the time goes:
time: 688 us; the launch traced here: 676 us
  other arithmetic  393 us (57%)
  matrix products  97.5 us (14%)
  waiting for transfers between devices  76 us (11%)
  local copies, waits for them, and re-layouts  71.3 us (10%)
  between operations  23.6 us (3%)
  starting transfers between devices  14.9 us (2%)
    another operation x43, other arithmetic, eliminate_one(): factor = jnp.linalg.cholesky(diag_block)  262 us
    another operation x10, other arithmetic, apply_inverse(): lax.linalg.triangular_solve(factor, halfway, left_side=True, lower=True,...  124 us
    ppermute x9, waiting for transfers between devices, shifted(): lax.ppermute(shard, axis, [(i, (i + by) % size) for i in range(size)])  51.1 us
    dot_general x21, matrix products, product(): jnp.dot(first_term, second_term, precision=lax.Precision.HIGHEST, preferr...  48.1 us
    another operation x40, local copies, waits for them, and re-layouts, apply_inverse(): lax.linalg.triangular_solve(factor, halfway, left_side=True, lower=True,...  26.8 us
    all_gather x1, waiting for transfers between devices, shards(): lax.all_gather(diag, 'rhs', axis=1, tiled=True)  20.3 us
    unnamed x96, local copies, waits for them, and re-layouts  18.5 us
    another operation x42, matrix products, apply_inverse(): lax.linalg.triangular_solve(factor, halfway, left_side=True, lower=True,...  17.2 us
  transfers between devices with their start and end apart: 16, of which 7 were waited for; matrix products, arithmetic and copies ran while one was open for 57% of the time, Pallas kernels for 0%

commit v1 on v0

--- a/solution.py
+++ b/solution.py
@@ -55,7 +55,9 @@
     column_start = lax.axis_index("rhs") * span_cols
     next_share = shifted(lower[:block_order], "tm", -1)
     full_diag, full_lower, next_lower = (
-        lax.all_gather(diag, "rhs", axis=1, tiled=True),
+        jnp.concatenate(
+            lax.all_to_all(jnp.stack([diag] * lax.axis_size("rhs")), "rhs", 0, 0), axis=1
+        ),
         lax.all_gather(lower, "rhs", axis=1, tiled=True),
         lax.all_gather(next_share, "rhs", axis=1, tiled=True),
     )

time: 688 us -> 667 us (0.969)
  waiting for transfers between devices: 76 us -> 52.4 us
    all_gather x1 -> x0, waiting for transfers between devices: 20.3 us -> none  [shards(): lax.all_gather(diag, 'rhs', axis=1, tiled=True)]
    unnamed x96 -> x103, local copies, waits for them, and re-layouts: 18.5 us -> 15.2 us
  transfers between devices with their start and end apart: 16 -> 16, of which waited for: 7 -> 6; matrix products, arithmetic and copies ran while one was open for 57% -> 79% of each run, Pallas kernels for 0% -> 0%
where the time goes in v1:
time: 667 us; the launch traced here: 654 us
  other arithmetic  389 us (58%)
  matrix products  95.4 us (14%)
  local copies, waits for them, and re-layouts  74.5 us (11%)
  waiting for transfers between devices  52.4 us (8%)
  between operations  23.8 us (4%)
  starting transfers between devices  19.2 us (3%)
    another operation x43, other arithmetic, eliminate_one(): factor = jnp.linalg.cholesky(diag_block)  255 us
    another operation x10, other arithmetic, apply_inverse(): lax.linalg.triangular_solve(factor, halfway, left_side=True, lower=True,...  123 us
    ppermute x9, waiting for transfers between devices, shifted(): lax.ppermute(shard, axis, [(i, (i + by) % size) for i in range(size)])  50.7 us
    dot_general x21, matrix products, product(): jnp.dot(first_term, second_term, precision=lax.Precision.HIGHEST, preferr...  48 us
    another operation x40, local copies, waits for them, and re-layouts, apply_inverse(): lax.linalg.triangular_solve(factor, halfway, left_side=True, lower=True,...  27 us
    another operation x42, matrix products, apply_inverse(): lax.linalg.triangular_solve(factor, stacked, left_side=True, lower=True)  17.4 us
    another operation x42, matrix products, apply_inverse(): lax.linalg.triangular_solve(factor, halfway, left_side=True, lower=True,...  16.6 us
    unnamed x103, local copies, waits for them, and re-layouts  15.2 us
  transfers between devices with their start and end apart: 16, of which 6 were waited for; matrix products, arithmetic and copies ran while one was open for 79% of the time, Pallas kernels for 0%

profile of v1, /device:TPU:0, one launch (start us, length us, event | category | flops | bytes accessed | tf_op | source)
XLA Modules:
  0.0 654.3 jit_solution(13338508129184685755)
XLA Ops:
  8.3 8.9 %collective-permute-start = (f32[512,256]{1,0:T(8,128)S(1)}, f32[512,256]{1,0:T(8,128)S(1)}, u32[]{:S(2)}, u32[]{:S(2)}) collective-permute-start(f32[512,256]{1,0:T(8,128)S(1)} %slice.279), channel_id=1, source_target_pairs={{0,254},{2,0},{4,2},{6,4},{8,6},{10,8},{12,10},{14,12},{16,14},{18... | collective-permute-start | bytes 1572872 | tf_op jit(solution)/shard_map/ppermute | solution.py:9
  17.2 11.2 %collective-permute-done = f32[512,256]{1,0:T(8,128)S(1)} collective-permute-done((f32[512,256]{1,0:T(8,128)S(1)}, f32[512,256]{1,0:T(8,128)S(1)}, u32[]{:S(2)}, u32[]{:S(2)}) %collective-permute-start) | collective-permute-done | bytes 524320 | tf_op jit(solution)/shard_map/ppermute | solution.py:9
  29.2 4.5 pad_maximum_fusion
  33.7 5.8 all-to-all-start
  44.7 3.9 fusion.293
  50.8 11.7 %cholesky.374 = f32[128,128]{1,0:T(8,128)S(1)} custom-call(f32[128,128]{1,0:T(8,128)S(1)} %cholesky.586), custom_call_target="Cholesky" | custom-call | tf_op jit(solution)/shard_map/jit(cholesky)/cholesky | solution.py:34
  62.6 9.8 %custom-call.46 = f32[1,128,128]{1,2,0:T(8,128)S(1)} custom-call(f32[1,128,128]{2,1,0:T(8,128)S(1)} %get-tuple-element.177), custom_call_target="InvertDiagBlocksLowerTriangular" | custom-call | tf_op jit(solution)/shard_map/jit(cholesky)/cholesky | solution.py:34
  73.8 12.5 %cholesky.393 = f32[128,128]{1,0:T(8,128)S(1)} custom-call(f32[128,128]{1,0:T(8,128)} %cholesky.590), custom_call_target="Cholesky" | custom-call | tf_op jit(solution)/shard_map/jit(cholesky)/cholesky | solution.py:34
  87.0 10.8 %custom-call.47 = f32[1,128,128]{1,2,0:T(8,128)S(1)} custom-call(f32[1,128,128]{2,1,0:T(8,128)} %get-tuple-element.174), custom_call_target="InvertDiagBlocksLowerTriangular" | custom-call | tf_op jit(solution)/shard_map/jit(cholesky)/cholesky | solution.py:34
  98.5 11.7 %cholesky.414 = f32[128,128]{1,0:T(8,128)S(1)} custom-call(f32[128,128]{1,0:T(8,128)S(1)} %cholesky.595), custom_call_target="Cholesky" | custom-call | tf_op jit(solution)/shard_map/jit(cholesky)/cholesky | solution.py:34
  110.9 9.8 %custom-call.48 = f32[1,128,128]{1,2,0:T(8,128)S(1)} custom-call(f32[1,128,128]{2,1,0:T(8,128)S(1)} %get-tuple-element.171), custom_call_target="InvertDiagBlocksLowerTriangular" | custom-call | tf_op jit(solution)/shard_map/jit(cholesky)/cholesky | solution.py:34
  121.3 11.9 %cholesky.431 = f32[128,128]{1,0:T(8,128)S(1)} custom-call(f32[128,128]{1,0:T(8,128)S(1)} %convolution_subtract_fusion.30), custom_call_target="Cholesky" | custom-call | tf_op jit(solution)/shard_map/jit(cholesky)/cholesky | solution.py:34
  137.4 7.9 %while.24 = (s32[]{:T(128)}, f32[512,512]{1,0:T(8,128)S(1)}, s32[4,2]{0,1:T(2,128)S(1)}, f32[4,128,128]{2,1,0:T(8,128)S(1)}, s32[]{:T(128)}) while((s32[]{:T(128)}, f32[512,512]{1,0:T(8,128)S(1)}, s32[4,2]{0,1:T(2,128)S(1)}, f32[4,128,128]{2,1,0:T(8,128)S(1)}, s32[]{:T(128)}) %tuple.119), condition=%wide.while_cond.1, body=%wide.while_body.1.sunk | while | flops 2 | bytes 131189 | solution.py:20
  147.6 11.7 %cholesky.446 = f32[128,128]{1,0:T(8,128)S(1)} custom-call(f32[128,128]{1,0:T(8,128)S(1)} %cholesky.599), custom_call_target="Cholesky" | custom-call | tf_op jit(solution)/shard_map/jit(cholesky)/cholesky | solution.py:34
  160.2 40.5 %custom-call.50 = f32[4,128,128]{1,2,0:T(8,128)S(1)} custom-call(f32[4,128,128]{2,1,0:T(8,128)} %copy-done.49), custom_call_target="InvertDiagBlocksLowerTriangular" | custom-call | tf_op jit(solution)/shard_map/triangular_solve/custom-call.8 | solution.py:20
  200.7 9.8 %custom-call.51 = f32[1,128,128]{1,2,0:T(8,128)S(1)} custom-call(f32[1,128,128]{2,1,0:T(8,128)S(1)} %get-tuple-element.167), custom_call_target="InvertDiagBlocksLowerTriangular" | custom-call | tf_op jit(solution)/shard_map/jit(cholesky)/cholesky | solution.py:34
  212.0 11.7 %cholesky.465 = f32[128,128]{1,0:T(8,128)S(1)} custom-call(f32[128,128]{1,0:T(8,128)S(1)} %cholesky.603), custom_call_target="Cholesky" | custom-call | tf_op jit(solution)/shard_map/jit(cholesky)/cholesky | solution.py:34
  223.8 9.8 %custom-call.52 = f32[1,128,128]{1,2,0:T(8,128)S(1)} custom-call(f32[1,128,128]{2,1,0:T(8,128)S(1)} %get-tuple-element.164), custom_call_target="InvertDiagBlocksLowerTriangular" | custom-call | tf_op jit(solution)/shard_map/jit(cholesky)/cholesky | solution.py:34
  235.8 13.3 %cholesky.486 = f32[128,128]{1,0:T(8,128)} custom-call(f32[128,128]{1,0:T(8,128)} %cholesky.608), custom_call_target="Cholesky" | custom-call | tf_op jit(solution)/shard_map/jit(cholesky)/cholesky | solution.py:34
  250.6 11.3 %custom-call.53 = f32[1,128,128]{1,2,0:T(8,128)} custom-call(f32[1,128,128]{2,1,0:T(8,128)} %get-tuple-element.161), custom_call_target="InvertDiagBlocksLowerTriangular" | custom-call | tf_op jit(solution)/shard_map/jit(cholesky)/cholesky | solution.py:34
  263.3 11.7 %cholesky.503 = f32[128,128]{1,0:T(8,128)S(1)} custom-call(f32[128,128]{1,0:T(8,128)S(1)} %convolution_subtract_fusion.29), custom_call_target="Cholesky" | custom-call | tf_op jit(solution)/shard_map/jit(cholesky)/cholesky | solution.py:34
  279.8 8.0 %while.25 = (s32[]{:T(128)}, f32[512,512]{1,0:T(8,128)S(1)}, s32[4,2]{0,1:T(2,128)S(1)}, f32[4,128,128]{2,1,0:T(8,128)S(1)}, s32[]{:T(128)}) while((s32[]{:T(128)}, f32[512,512]{1,0:T(8,128)S(1)}, s32[4,2]{0,1:T(2,128)S(1)}, f32[4,128,128]{2,1,0:T(8,128)S(1)}, s32[]{:T(128)}) %tuple.140), condition=%wide.while_cond.1.clone, body=%wide.while_body.1.clone.sunk | while | flops 2 | bytes 131189 | solution.py:20
  287.8 39.5 %custom-call.55 = f32[4,128,128]{1,2,0:T(8,128)S(1)} custom-call(f32[4,128,128]{2,1,0:T(8,128)S(1)} %get-tuple-element.92), custom_call_target="InvertDiagBlocksLowerTriangular" | custom-call | tf_op jit(solution)/shard_map/triangular_solve/custom-call.8 | solution.py:20
  327.3 2.6 copy.16
  330.0 1.9 dynamic-slice_bitcast_fusion.1
  331.9 2.2 fusion.294
  359.8 1.9 fusion.1
  361.7 2.2 fusion.296
  364.0 3.2 fusion.3
  367.3 17.1 %collective-permute-done.2 = f32[512,256]{0,1:T(8,128)} collective-permute-done((f32[512,256]{0,1:T(8,128)}, f32[512,256]{0,1:T(8,128)}, u32[]{:S(2)}, u32[]{:S(2)}) %collective-permute-start.2) | collective-permute-done | bytes 524320 | tf_op jit(solution)/shard_map/ppermute | solution.py:9
  384.4 4.0 fusion
  390.2 2.6 copy.8
  394.3 2.1 collective-permute-start.6
  396.8 2.7 convolution_subtract_fusion.22
  399.5 4.0 collective-permute-done.3
  403.6 2.4 convolution_subtract_fusion.27
  406.0 3.1 convolution_subtract_fusion.25
  409.1 2.0 fusion.9
  411.1 3.3 fusion.6
  414.4 2.7 copy.17
  419.7 11.7 %cholesky.518 = f32[128,128]{1,0:T(8,128)S(1)} custom-call(f32[128,128]{1,0:T(8,128)S(1)} %cholesky.612), custom_call_target="Cholesky" | custom-call | tf_op jit(solution)/shard_map/jit(cholesky)/cholesky | solution.py:34
  432.1 10.4 %custom-call.56 = f32[1,128,128]{1,2,0:T(8,128)} custom-call(f32[1,128,128]{2,1,0:T(8,128)S(1)} %get-tuple-element.157), custom_call_target="InvertDiagBlocksLowerTriangular" | custom-call | tf_op jit(solution)/shard_map/jit(cholesky)/cholesky | solution.py:34
  447.3 13.6 %cholesky.537 = f32[128,128]{1,0:T(8,128)} custom-call(f32[128,128]{1,0:T(8,128)} %cholesky.616), custom_call_target="Cholesky" | custom-call | tf_op jit(solution)/shard_map/jit(cholesky)/cholesky | solution.py:34
  463.0 11.3 %custom-call.57 = f32[1,128,128]{1,2,0:T(8,128)} custom-call(f32[1,128,128]{2,1,0:T(8,128)} %get-tuple-element.154), custom_call_target="InvertDiagBlocksLowerTriangular" | custom-call | tf_op jit(solution)/shard_map/jit(cholesky)/cholesky | solution.py:34
  478.0 13.2 %cholesky.558 = f32[128,128]{1,0:T(8,128)} custom-call(f32[128,128]{1,0:T(8,128)} %cholesky.621), custom_call_target="Cholesky" | custom-call | tf_op jit(solution)/shard_map/jit(cholesky)/cholesky | solution.py:34
  493.4 11.3 %custom-call.58 = f32[1,128,128]{1,2,0:T(8,128)} custom-call(f32[1,128,128]{2,1,0:T(8,128)} %get-tuple-element.151), custom_call_target="InvertDiagBlocksLowerTriangular" | custom-call | tf_op jit(solution)/shard_map/jit(cholesky)/cholesky | solution.py:34
  507.5 13.3 %cholesky.575 = f32[128,128]{1,0:T(8,128)} custom-call(f32[128,128]{1,0:T(8,128)} %convolution_subtract_fusion.28), custom_call_target="Cholesky" | custom-call | tf_op jit(solution)/shard_map/jit(cholesky)/cholesky | solution.py:34
  527.3 10.5 %while.26 = (s32[]{:T(128)}, f32[512,512]{1,0:T(8,128)S(1)}, s32[4,2]{0,1:T(2,128)S(1)}, f32[4,128,128]{2,1,0:T(8,128)}, s32[]{:T(128)}) while((s32[]{:T(128)}, f32[512,512]{1,0:T(8,128)S(1)}, s32[4,2]{0,1:T(2,128)S(1)}, f32[4,128,128]{2,1,0:T(8,128)}, s32[]{:T(128)}) %tuple.141), condition=%wide.while_cond.1.clone.1, body=%wide.while_body.1.clone.1.sunk | while | flops 2 | bytes 132205 | solution.py:20
  527.9 2.0 bitcast_dynamic-update-slice_fusion.8
  530.6 2.0 bitcast_dynamic-update-slice_fusion.8
  533.2 2.0 bitcast_dynamic-update-slice_fusion.8
  535.8 2.0 bitcast_dynamic-update-slice_fusion.8
  537.8 40.8 %custom-call.60 = f32[4,128,128]{1,2,0:T(8,128)} custom-call(f32[4,128,128]{2,1,0:T(8,128)} %get-tuple-element.94), custom_call_target="InvertDiagBlocksLowerTriangular" | custom-call | tf_op jit(solution)/shard_map/triangular_solve/custom-call.8 | solution.py:20
  578.6 2.0 constant_dynamic-slice_fusion.3
  580.5 2.3 convolution_subtract_fusion.21
  593.4 2.0 convolution_subtract_fusion.20
  610.2 2.0 fusion.297
  612.5 2.3 fusion.10
  616.5 2.1 fusion.5
  619.7 2.5 collective-permute-done.7
  622.2 3.1 convolution_subtract_fusion.23
  625.3 15.8 %collective-permute-done.4 = f32[512,256]{0,1:T(8,128)} collective-permute-done((f32[512,256]{0,1:T(8,128)S(1)}, f32[512,256]{0,1:T(8,128)}, u32[]{:S(2)}, u32[]{:S(2)}) %collective-permute-start.4) | collective-permute-done | bytes 524320 | tf_op jit(solution)/shard_map/ppermute | solution.py:9
  641.1 2.1 convolution_subtract_fusion
  644.2 2.9 convolution_negate_fusion
  (339 shorter events, 125.9 us)
Async XLA Ops:
  7.2 322.8 %all-gather.9.cloned.1.call-start = ((), (), s32[]{:S(2)}) async-start(), calls=%async_computation.2 | async-start | bytes 1572864 | tf_op jit(solution)/shard_map/all_gather | solution.py:62
  8.3 20.1 %collective-permute-start = (f32[512,256]{1,0:T(8,128)S(1)}, f32[512,256]{1,0:T(8,128)S(1)}, u32[]{:S(2)}, u32[]{:S(2)}) collective-permute-start(f32[512,256]{1,0:T(8,128)S(1)} %slice.279), channel_id=1, source_target_pairs={{0,254},{2,0},{4,2},{6,4},{8,6},{10,8},{12,10},{14,12},{16,14},{18... | collective-permute-start | bytes 1572872 | tf_op jit(solution)/shard_map/ppermute | solution.py:9
  28.3 0.8 copy-start.42
  33.7 5.8 copy-start.17
  33.7 11.0 %all-to-all-start = ((f32[2,2048,256]{2,1,0:T(8,128)}), f32[2,2048,256]{2,1,0:T(8,128)}, u32[]{:S(2)}, u32[]{:S(2)}) async-start(f32[2,2048,256]{2,1,0:T(8,128)} %pad_maximum_fusion), calls=%async_computation | async-start | bytes 8388608 | tf_op jit(solution)/shard_map/all_to_all | solution.py:59
  39.4 292.4 %all-gather.7.cloned.1.call-start = ((), (), s32[]{:S(2)}) async-start(), calls=%async_computation.1 | async-start | bytes 6291456 | tf_op jit(solution)/shard_map/all_gather | solution.py:61
  41.3 1.0 copy-start.34
  41.3 373.0 %all-gather.13.cloned.1.call-start = ((), (), s32[]{:S(2)}) async-start(), calls=%async_computation.4 | async-start | bytes 1572864 | tf_op jit(solution)/shard_map/all_gather | solution.py:101
  49.9 1.0 copy-start.21
  50.8 21.7 %copy-start.22 = (f32[512,512]{1,0:T(8,128)S(1)}, f32[512,512]{1,0:T(8,128)}, u32[]{:S(2)}) copy-start(f32[512,512]{1,0:T(8,128)} %copy-done.21) | copy-start | bytes 3145732
  145.3 0.7 copy-start.49
  146.6 1.0 copy-start.18
  147.6 63.1 %copy-start.19 = (f32[512,512]{1,0:T(8,128)S(1)}, f32[512,512]{1,0:T(8,128)}, u32[]{:S(2)}) copy-start(f32[512,512]{1,0:T(8,128)} %copy-done.18) | copy-start | bytes 3145732
  211.3 0.7 copy-start.40
  327.3 25.8 %copy-start.13 = (f32[4,128,128]{1,2,0:T(8,128)}, f32[4,128,128]{1,2,0:T(8,128)S(1)}, u32[]{:S(2)}) copy-start(f32[4,128,128]{1,2,0:T(8,128)S(1)} %custom-call.55) | copy-start | bytes 786436
  335.7 2.1 copy-start.38
  346.3 1.5 copy-start.9
  347.6 0.8 copy-start.23
  347.7 1.2 copy-start.31
  347.7 1.3 copy-start.32
  347.7 1.3 copy-start.43
  348.4 11.3 %copy-start.7 = (f32[512,576]{0,1:T(8,128)}, f32[512,576]{0,1:T(8,128)S(1)}, u32[]{:S(2)}) copy-start(f32[512,576]{0,1:T(8,128)S(1)} %pad_maximum_fusion.2) | copy-start | bytes 3538948
  353.9 2.0 copy-start.14
  355.9 2.5 copy-start.28
  356.3 1.4 copy-start.11
  356.3 2.4 copy-start
  357.6 0.7 copy-start.25
  358.4 1.4 copy-start.8
  361.7 216.9 %all-gather.11.cloned.1.call-start = ((), (), s32[]{:S(2)}) async-start(), calls=%async_computation.3 | async-start | bytes 1572864 | tf_op jit(solution)/shard_map/all_gather | solution.py:103
  364.0 20.4 %collective-permute-start.2 = (f32[512,256]{0,1:T(8,128)}, f32[512,256]{0,1:T(8,128)}, u32[]{:S(2)}, u32[]{:S(2)}) collective-permute-start(f32[512,256]{0,1:T(8,128)} %get-tuple-element.145), channel_id=1, source_target_pairs={{0,2},{2,4},{4,6},{6,8},{8,10},{10,12},{12,14},{14,16},{16,18},{18... | collective-permute-start | bytes 1572872 | tf_op jit(solution)/shard_map/ppermute | solution.py:9
  367.2 215.6 %all-gather.15.cloned.1.call-start = ((), (), s32[]{:S(2)}) async-start(), calls=%async_computation.5 | async-start | bytes 1572864 | tf_op jit(solution)/shard_map/all_gather | solution.py:104
  388.4 15.1 %collective-permute-start.3 = (f32[512,256]{1,0:T(8,128)}, f32[512,256]{1,0:T(8,128)}, u32[]{:S(2)}, u32[]{:S(2)}) collective-permute-start(f32[512,256]{1,0:T(8,128)} %fusion), channel_id=1, source_target_pairs={{0,254},{2,0},{4,2},{6,4},{8,6},{10,8},{12,10},{14,12},{16,14},{18... | collective-permute-start | bytes 1572872 | tf_op jit(solution)/shard_map/ppermute | solution.py:9
  390.2 202.7 %collective-permute-start.8 = (f32[64,512]{1,0:T(8,128)}, f32[64,512]{1,0:T(8,128)}, u32[]{:S(2)}, u32[]{:S(2)}) collective-permute-start(f32[64,512]{1,0:T(8,128)} %param.16), channel_id=1, source_target_pairs={{0,254},{2,0},{4,2},{6,4},{8,6},{10,8},{12,10},{14,12},{16,14},{18... | collective-permute-start | bytes 393224 | tf_op jit(solution)/shard_map/ppermute | solution.py:9
  392.8 3.9 copy-start.10
  392.8 3.9 copy-start.24
  392.8 4.0 copy-start.36
  394.3 218.2 %collective-permute-start.6 = (f32[512,64]{0,1:T(8,128)}, f32[512,64]{0,1:T(8,128)}, u32[]{:S(2)}, u32[]{:S(2)}) collective-permute-start(f32[512,64]{0,1:T(8,128)} %pad_maximum_fusion.9), channel_id=1, source_target_pairs={{0,2},{2,4},{4,6},{6,8},{8,10},{10,12},{12,14},{14,16},{16,18},{18... | collective-permute-start | bytes 393224 | tf_op jit(solution)/shard_map/ppermute | solution.py:9
  396.4 220.0 %collective-permute-start.1 = (f32[512,256]{0,1:T(8,128)}, f32[512,256]{0,1:T(8,128)}, u32[]{:S(2)}, u32[]{:S(2)}) collective-permute-start(f32[512,256]{0,1:T(8,128)} %get-tuple-element.144), channel_id=1, source_target_pairs={{0,2},{2,4},{4,6},{6,8},{8,10},{10,12},{12,14},{14,16},{16,18},{18... | collective-permute-start | bytes 1572872 | tf_op jit(solution)/shard_map/ppermute | solution.py:9
  396.8 6.8 %copy-start.35 = (f32[64,2048]{1,0:T(8,128)S(1)}, f32[64,2048]{1,0:T(8,128)}, u32[]{:S(2)}) copy-start(f32[64,2048]{1,0:T(8,128)} %param.15) | copy-start | bytes 1572868
  403.5 216.2 %all-gather.17.cloned.1.call-start = ((), (), s32[]{:S(2)}) async-start(), calls=%async_computation.6 | async-start | bytes 1572864 | tf_op jit(solution)/shard_map/all_gather | solution.py:102
  406.0 5.1 copy-start.29
  414.4 2.7 copy-start.12
  418.6 1.1 copy-start.20
  431.4 0.8 copy-start.48
  521.8 3.4 copy-start.6
  537.8 40.8 %copy-start.4 = (f32[512,512]{1,0:T(8,128)}, f32[512,512]{1,0:T(8,128)S(1)}, u32[]{:S(2)}) copy-start(f32[512,512]{1,0:T(8,128)S(1)} %get-tuple-element.335) | copy-start | bytes 3145732
  578.5 2.0 copy-start.2
  582.9 1.2 copy-start.33
  584.1 0.9 copy-start.16
  584.1 1.3 copy-start.5
  592.1 1.3 copy-start.27
  592.1 1.3 copy-start.47
  592.8 5.9 copy-start.1
  595.8 2.9 copy-start.46
  601.4 3.0 copy-start.26
  602.7 3.4 copy-start.15
  610.1 2.4 copy-start.44
  610.1 12.1 %collective-permute-start.7 = (f32[512,64]{0,1:T(8,128)}, f32[512,64]{0,1:T(8,128)}, u32[]{:S(2)}, u32[]{:S(2)}) collective-permute-start(f32[512,64]{0,1:T(8,128)} %pad_maximum_fusion.7), channel_id=1, source_target_pairs={{0,2},{2,4},{4,6},{6,8},{8,10},{10,12},{12,14},{14,16},{16,18},{18... | collective-permute-start | bytes 393224 | tf_op jit(solution)/shard_map/ppermute | solution.py:9
  610.1 34.1 %collective-permute-start.5 = (f32[512,256]{0,1:T(8,128)}, f32[512,256]{0,1:T(8,128)}, u32[]{:S(2)}, u32[]{:S(2)}) collective-permute-start(f32[512,256]{0,1:T(8,128)} %get-tuple-element.142), channel_id=1, source_target_pairs={{0,2},{2,4},{4,6},{6,8},{8,10},{10,12},{12,14},{14,16},{16,18},{18... | collective-permute-start | bytes 1572872 | tf_op jit(solution)/shard_map/ppermute | solution.py:9
  610.1 31.0 %collective-permute-start.4 = (f32[512,256]{0,1:T(8,128)S(1)}, f32[512,256]{0,1:T(8,128)}, u32[]{:S(2)}, u32[]{:S(2)}) collective-permute-start(f32[512,256]{0,1:T(8,128)S(1)} %get-tuple-element.143), channel_id=1, source_target_pairs={{0,2},{2,4},{4,6},{6,8},{8,10},{10,12},{12,14},{14,16},{16,18},{18... | collective-permute-start | bytes 1572872 | tf_op jit(solution)/shard_map/ppermute | solution.py:9
  615.1 1.4 copy-start.30
  616.4 2.4 copy-start.37
  618.6 3.6 copy-start.45
  619.7 21.4 %copy-start.3 = (f32[512,512]{1,0:T(8,128)S(1)}, f32[512,512]{1,0:T(8,128)}, u32[]{:S(2)}) copy-start(f32[512,512]{1,0:T(8,128)} %all-gather.17.cloned.1.call-done) | copy-start | bytes 3145732
  (2 other events, 1.3 us)
Sparse Core Ops, SparseCore 0:
  29.3 14.0 all-gather.8
  45.1 19.7 all-gather.6
  361.8 13.2 all-gather.12
  377.3 15.6 all-gather.10
  403.7 12.2 all-gather.14
  418.1 15.7 all-gather.16
